TPU v7x, 32 devices: a whole 2x2x4 slice. The times are simulated.
32 devices in a mesh: tm: 8 (over z, core), mp: 2 (over y), batch: 2 (over x).
Axes of the slice: x: 2, y: 2, z: 4, core: 2. Of those that a mesh axis runs over, the one named last changes fastest.
Arguments:
- frames: bfloat16 [16384, 1024], P(('batch', 'tm')), parts along dimension 0, may hold values from -40 to 40
- norm_gain: float32 [1024], replicated, may hold values from 0.5 to 1.5
- qkv_weight: bfloat16 [3, 1024, 1024], P(None, None, 'mp'), may hold values from -2 to 2
- out_weight: bfloat16 [1024, 1024], P('mp'), may hold values from -0.1875 to 0.1875
- cotangent: bfloat16 [16384, 1024], P(('batch', 'tm')), parts along dimension 0, may hold values from -6 to 6
- pad_mask: int32 [16384], P('batch'), parts along dimension 0, may hold values from 0 to 1, as said below
- utt_lengths: int32 [16], P('batch'), parts along dimension 0, may hold values from 1 to 2048, 8192 in all
Outputs:
- frame_grad: bfloat16 [16384, 1024], P(('batch', 'tm'), 'mp'), parts along dimension 0
- qkv_grad: float32 [6, 1024, 1024], P('batch', 'tm', 'mp'), parts along dimension 0
- out_grad: float32 [2048, 1024], P(('batch', 'mp'), 'tm'), parts along dimension 0
There are 2 independent parts, one for each index of `batch`. A program takes and returns all parts, laid end to end along the dimension named above; an argument that names none is the same for every part. Nothing has to cross between parts.
Inputs may be any that keep to these rules, and one draw needn't show every extreme that they name: `pad_mask`: in each aligned block of 256 frames, the padding frames form the tail of the block, fewer than 128 of them. `utt_lengths`: 8 lengths that sum to 8192; the largest is exactly 2048.
All inputs are finite; a program needn't handle non-finite values.
Results may differ from a plain program's by a relative error of at most 0.012.
The roundings to bfloat16 on the way count: a program that leaves them out, or rounds other values in their place, can miss the bound.
Values may be sent and summed in bfloat16 or wider, within the bound.
A program may use at most 128 MiB of HBM per device.

v0:
```python
import jax
import jax.numpy as jnp
from jax import lax
from jax.sharding import PartitionSpec as P

HS = 128
CH = 32
EPSILON = 1e-05


def with_halo(block, sides, width):
    for axis, dim in sides:
        count = lax.axis_size(axis)
        forward = [(i, i + 1) for i in range(count - 1)]
        backward = [(target, source) for source, target in forward]
        low = lax.ppermute(
            lax.slice_in_dim(block, block.shape[dim] - width, None, axis=dim), axis, forward
        )
        high = lax.ppermute(lax.slice_in_dim(block, 0, width, axis=dim), axis, backward)
        block = jnp.concatenate([low, block, high], axis=dim)
    return block


def layer_norm(frames, norm_gain):
    values = frames.astype(jnp.float32)
    center = values - jnp.mean(values, axis=-1, keepdims=True)
    inverse = lax.rsqrt(jnp.mean(center * center, axis=-1, keepdims=True) + EPSILON)
    normal_form = center * inverse
    return (normal_form, inverse, (normal_form * norm_gain).astype(jnp.bfloat16))


def norm_backward(incoming, normal_form, inverse, norm_gain):
    scaled = incoming * norm_gain
    mean_grad = jnp.mean(scaled, axis=-1, keepdims=True)
    mean_proj = jnp.mean(scaled * normal_form, axis=-1, keepdims=True)
    return inverse * (scaled - mean_grad - normal_form * mean_proj)


def windows(block_rows):
    block_count = block_rows.shape[0] - 2
    return jnp.concatenate(
        [block_rows[:block_count], block_rows[1 : block_count + 1], block_rows[2:]], axis=1
    )


def fold_keys(window):
    block_width = window.shape[1] // 3
    trailing = [(0, 0)] * (window.ndim - 1)
    pieces = [
        jnp.pad(
            window[:, offset * block_width : (offset + 1) * block_width],
            [(offset, 2 - offset)] + trailing,
        )
        for offset in range(3)
    ]
    return pieces[0] + pieces[1] + pieces[2]


def permitted(query_start, query_count, key_start, key_count, pad_mask, utt_lengths):
    utt_ends = jnp.cumsum(utt_lengths)
    query_pos = query_start + jnp.arange(query_count, dtype=jnp.int32)
    key_pos = key_start + jnp.arange(key_count, dtype=jnp.int32)

    def segment(positions):
        return jnp.sum((utt_ends[None, :] <= positions[:, None]).astype(jnp.int32), axis=1)

    padded = jnp.pad(pad_mask, 2 * CH)
    live_keys = lax.dynamic_slice(
        padded, (jnp.asarray(key_start + 2 * CH, jnp.int32),), (key_count,)
    )
    query_cells = query_pos.reshape(-1, CH)
    query_seg = segment(query_pos).reshape(-1, CH)
    key_cells = windows(key_pos.reshape(-1, CH))
    key_seg = windows(segment(key_pos).reshape(-1, CH))
    key_live = windows(live_keys.reshape(-1, CH))
    same_utt = query_seg[:, :, None] == key_seg[:, None, :]
    return same_utt & (
        (key_live[:, None, :] == 1) | (query_cells[:, :, None] == key_cells[:, None, :])
    )


def attend(queries, grad_rows, key_blocks, value_blocks, allowed):
    score_scale = HS ** (-0.5)
    key_win = windows(key_blocks)
    value_win = windows(value_blocks)
    scores = (
        jnp.einsum("cihd,cjhd->chij", queries, key_win, preferred_element_type=jnp.float32)
        * score_scale
    )
    scores = jnp.where(allowed[:, None], scores, -1e30)
    row_max = jnp.max(scores, axis=-1, keepdims=True)
    weights = jnp.exp(scores - row_max)
    attn_probs = weights / jnp.sum(weights, axis=-1, keepdims=True)
    rounded = attn_probs.astype(jnp.bfloat16)
    mixed_out = jnp.einsum(
        "chij,cjhd->cihd", rounded, value_win, preferred_element_type=jnp.float32
    ).astype(jnp.bfloat16)
    prob_grad = jnp.einsum(
        "cihd,cjhd->chij", grad_rows, value_win, preferred_element_type=jnp.float32
    )
    centre = jnp.sum(attn_probs * prob_grad, axis=-1, keepdims=True)
    score_grad = (attn_probs * (prob_grad - centre) * score_scale).astype(jnp.bfloat16)
    query_grad = jnp.einsum(
        "chij,cjhd->cihd", score_grad, key_win, preferred_element_type=jnp.float32
    )
    key_grad = fold_keys(
        jnp.einsum("chij,cihd->cjhd", score_grad, queries, preferred_element_type=jnp.float32)
    )
    value_grad = fold_keys(
        jnp.einsum("chij,cihd->cjhd", rounded, grad_rows, preferred_element_type=jnp.float32)
    )
    return (mixed_out, query_grad, key_grad, value_grad)


def on_device(frames, norm_gain, qkv_weight, out_weight, cotangent, pad_mask, utt_lengths):
    frame_rows = frames.shape[0]
    head_cols = qkv_weight.shape[2]
    heads_here = head_cols // HS
    first_row = lax.axis_index("tm") * frame_rows
    normal_form, inverse, normed = layer_norm(frames, norm_gain)
    projected = jnp.einsum(
        "rd,mdh->mrh", normed, qkv_weight, preferred_element_type=jnp.float32
    ).astype(jnp.bfloat16)
    live_rows = lax.dynamic_slice(pad_mask, (first_row,), (frame_rows,))
    masked = cotangent * live_rows.astype(jnp.bfloat16)[:, None]
    grad_heads = jnp.dot(masked, out_weight.T, preferred_element_type=jnp.float32).astype(
        jnp.bfloat16
    )

    def blocks(tensor):
        return tensor.reshape(-1, CH, heads_here, HS)

    stacked = jnp.concatenate([projected, grad_heads[None]], axis=0)
    extended = with_halo(stacked, (("tm", 1),), 2 * CH)
    query_rim = extended[:, CH:-CH]
    allowed = permitted(
        first_row - CH,
        frame_rows + 2 * CH,
        first_row - 2 * CH,
        frame_rows + 4 * CH,
        pad_mask,
        utt_lengths,
    )
    mixed_ext, query_ext, key_ext, value_ext = attend(
        blocks(query_rim[0]),
        blocks(query_rim[3]),
        blocks(extended[1]),
        blocks(extended[2]),
        allowed,
    )
    mixed_out = mixed_ext[1:-1]
    query_grad = query_ext[1:-1]
    key_grad = key_ext[2:-2]
    value_grad = value_ext[2:-2]
    all_grads = (
        jnp.stack([query_grad, key_grad, value_grad])
        .reshape(3, frame_rows, head_cols)
        .astype(jnp.bfloat16)
    )
    mixed_rows = mixed_out.reshape(frame_rows, head_cols)
    weight_terms = jnp.einsum("rd,mrh->mdh", normed, all_grads, preferred_element_type=jnp.float32)
    out_terms = jnp.einsum("rh,rd->hd", mixed_rows, masked, preferred_element_type=jnp.float32)
    qkv_grad, out_grad = (
        lax.psum_scatter(weight_terms, "tm", scatter_dimension=1, tiled=True),
        lax.psum_scatter(out_terms, "tm", scatter_dimension=1, tiled=True),
    )
    incoming = jnp.einsum("mrh,mdh->rd", all_grads, qkv_weight, preferred_element_type=jnp.float32)
    head_total = lax.psum(incoming, "mp")
    full_grad = norm_backward(head_total, normal_form, inverse, norm_gain)
    share_cols = full_grad.shape[1] // lax.axis_size("mp")
    frame_grad = lax.dynamic_slice_in_dim(
        full_grad, lax.axis_index("mp") * share_cols, share_cols, 1
    )
    return (frame_grad.astype(jnp.bfloat16), qkv_grad, out_grad)


def solution(mesh):
    placed = (
        P(("batch", "tm"), None),
        P(),
        P(None, None, "mp"),
        P("mp", None),
        P(("batch", "tm"), None),
        P("batch"),
        P("batch"),
    )
    return jax.shard_map(
        on_device,
        mesh=mesh,
        in_specs=placed,
        out_specs=(P(("batch", "tm"), "mp"), P("batch", "tm", "mp"), P(("batch", "mp"), "tm")),
        check_vma=False,
    )
```

profile of v0, /device:TPU:0, one launch (start us, length us, event | category | flops | bytes accessed | tf_op | source)
XLA Modules:
  0.0 311.9 jit_solution(12134649921171048453)
XLA Ops:
  11.2 3.3 %fusion.34 = bf16[1,1024,512]{2,1,0:T(8,128)(2,1)S(1)} fusion(bf16[512,1024]{1,0:T(8,128)(2,1)} %param.10, bf16[1024,1024]{1,0:T(8,128)(2,1)} %param.11, bf16[1024]{0:T(1024)(128)(2,1)S(1)} %dynamic-slice_convert_fusion), kind=kOutput, calls=%fused_computation.43 | convolution fusion | flops 1075314688 | bytes 4196352 | tf_op jit(solution)/shard_map/dot_general | solution.py:126
  14.6 4.0 %convert_bitcast_fusion = bf16[3,1024,512]{2,1,0:T(8,128)(2,1)S(1)} fusion(bf16[3,1024,512]{2,1,0:T(8,128)(2,1)S(1)} %copy-done, f32[1024]{0:T(1024)S(1)} %copy-done.22, bf16[1024,1024]{1,0:T(8,128)(2,1)S(1)} %copy-done.3, f32[1024]{0:T(1024)S(1)} %add_rsqrt_fusion, f32[1024]{0:T(1024)S(1)} %broadcast_multiply_fusion.3), kind=kOutput, calls=%fused_computation.9 | convolution fusion | flops 3228041216 | bytes 8400896 | tf_op jit(solution)/shard_map/rd,mdh->mrh/dot_general | solution.py:121
  21.7 3.7 %collective-permute-start = (bf16[4,64,512]{2,1,0:T(8,128)(2,1)}, bf16[4,64,512]{2,1,0:T(8,128)(2,1)}, u32[]{:S(2)}, u32[]{:S(2)}) collective-permute-start(bf16[4,64,512]{2,1,0:T(8,128)(2,1)} %get-tuple-element.30), channel_id=1, source_target_pairs={{0,4},{4,8},{8,12},{12,16},{16,20},{20,24},{24,28},{1,5},{5,9},{9,... | collective-permute-start | bytes 786440 | tf_op jit(solution)/shard_map/ppermute | solution.py:16
  33.4 3.2 %pad_maximum_fusion = (bf16[1,1088,512]{2,1,0:T(8,128)(2,1)}, bf16[1,1088,512]{2,1,0:T(8,128)(2,1)}, bf16[1,1088,512]{2,1,0:T(8,128)(2,1)}) fusion(bf16[4,64,512]{2,1,0:T(8,128)(2,1)S(1)} %collective-permute-done.1, bf16[1,1024,512]{2,1,0:T(8,128)(2,1)} %copy-done.4, bf16[3,1024,512]{2,1,0:T(8,128)(2,1)} %copy-done.1, ...), kind=kLoop, calls=%fused_computation.44 | loop fusion | flops 10027008 | bytes 8060928 | tf_op jit(solution)/shard_map/concatenate | solution.py:20
  36.7 3.1 slice.216
  39.8 4.2 %pad_maximum_fusion.11 = (bf16[1,1088,512]{2,1,0:T(8,128)(2,1)}, bf16[1,1088,512]{2,1,0:T(8,128)(2,1)}, bf16[1,1088,512]{2,1,0:T(8,128)(2,1)}, bf16[1,1088,512]{2,1,0:T(8,128)(2,1)}, bf16[1,1088,512]{2,1,0:T(8,128)(2,1)}) fusion(bf16[4,64,512]{2,1,0:T(8,128)(2,1)S(1)} %collective-permute-done.1, bf16[4,64,512]{2,1,0:T(8,128)(2,1)} %collective-permute-done, ...), kind=kLoop, calls=%fused_computation.55 | loop fusion | flops 21168128 | bytes 10289152 | tf_op jit(solution)/shard_map/slice | solution.py:145
  44.0 3.1 reshape_squeeze.8
  47.1 3.1 reshape_squeeze.9
  50.2 3.1 slice.194
  53.3 3.1 slice.214
  56.4 3.1 slice.191
  59.4 3.1 slice.196
  62.5 3.1 slice.212
  69.0 3.2 %fusion.47 = f32[34,4,32,96]{3,2,1,0:T(8,128)} fusion(bf16[34,96,4,128]{3,1,2,0:T(8,128)(2,1)S(1)} %copy_dynamic-update-slice_fusion, bf16[34,32,4,128]{3,2,1,0:T(4,128)(2,1)S(1)} %copy-done.8), kind=kOutput, calls=%fused_computation.73 | convolution fusion | flops 106954752 | bytes 6127616 | tf_op jit(solution)/shard_map/cihd,cjhd->chij/dot_general | solution.py:98
  75.6 2.2 fusion.69
  77.8 28.3 %fusion.31 = bf16[34,32,4,128]{3,1,2,0:T(8,128)(2,1)} fusion(bf16[34,96,4,128]{3,1,2,0:T(8,128)(2,1)} %copy-done.6, f32[34,4,32,96]{3,2,1,0:T(8,128)} %fusion.47, f32[34,4,32,96]{3,2,1,0:T(8,128)} %get-tuple-element.42, f32[34,4,32]{2,1,0:T(4,128)S(1)} %get-tuple-element.41), kind=kOutput, calls=%fused_computation.42 | convolution fusion | flops 110440800 | bytes 7816192 | tf_op jit(solution)/shard_map/chij,cjhd->cihd/dot_general | solution.py:103
  106.1 31.5 %convolution_bitcast_fusion.1 = f32[34,96,4,128]{3,1,2,0:T(8,128)} fusion(f32[34,4,32,96]{3,2,1,0:T(8,128)} %fusion.47, bf16[34,32,4,128]{3,2,1,0:T(4,128)(2,1)} %reshape_squeeze.8, f32[34,4,32,96]{3,2,1,0:T(8,128)} %get-tuple-element.42, f32[34,4,32]{2,1,0:T(4,128)S(1)} %get-tuple-element.41), kind=kOutput, calls=%fused_computation.11 | convolution fusion | flops 109883744 | bytes 11158528 | tf_op jit(solution)/shard_map/chij,cihd->cjhd/dot_general | solution.py:107
  137.6 13.4 %convolution_bitcast_fusion = f32[34,96,4,128]{3,1,2,0:T(8,128)} fusion(bf16[34,32,4,128]{3,2,1,0:T(4,128)(2,1)} %reshape_squeeze.9, f32[34,4,32]{2,1,0:T(4,128)S(1)} %get-tuple-element.41, f32[34,4,32,96]{3,2,1,0:T(8,128)} %copy-done.5, pred[34,32,96]{2,1,0:T(8,128)(4,1)S(1)} %or_and_fusion), kind=kOutput, calls=%fused_computation.10 | convolution fusion | flops 109048160 | bytes 9591808 | tf_op jit(solution)/shard_map/chij,cihd->cjhd/dot_general | solution.py:110
  153.8 2.2 stack.12
  156.0 3.8 %fusion.66 = (f32[34,32,4,128]{3,1,2,0:T(8,128)S(1)}, f32[34,32,4,128]{3,1,2,0:T(8,128)S(1)}, f32[34,32,4,128]{3,1,2,0:T(8,128)S(1)}) fusion(f32[34,96,4,128]{3,1,2,0:T(8,128)} %convolution_bitcast_fusion.1), kind=kLoop, calls=%fused_computation.111 | loop fusion | bytes 13369344 | tf_op jit(solution)/shard_map/slice | solution.py:51
  162.1 2.3 stack.13
  164.4 2.3 constant_dynamic-update-slice_fusion.2
  166.6 3.8 %fusion.65 = (f32[34,32,4,128]{3,1,2,0:T(8,128)S(1)}, f32[34,32,4,128]{3,1,2,0:T(8,128)S(1)}, f32[34,32,4,128]{3,1,2,0:T(8,128)S(1)}) fusion(f32[34,96,4,128]{3,1,2,0:T(8,128)} %convolution_bitcast_fusion), kind=kLoop, calls=%fused_computation.110 | loop fusion | bytes 13369344 | tf_op jit(solution)/shard_map/slice | solution.py:51
  172.7 2.4 stack.14
  175.2 2.4 constant_dynamic-update-slice_fusion.1
  178.6 6.9 %convolution_bitcast_fusion.3 = f32[1024,1024]{1,0:T(8,128)} fusion(bf16[3,1024,512]{2,1,0:T(8,128)(2,1)} %constant_dynamic-update-slice_fusion, bf16[3,1024,512]{2,1,0:T(8,128)(2,1)S(1)} %copy-done), kind=kOutput, calls=%fused_computation.18 | convolution fusion | flops 3221225472 | bytes 10485760 | tf_op jit(solution)/shard_map/mrh,mdh->rd/dot_general | solution.py:167
  186.2 8.8 %convolution_bitcast_fusion.2 = f32[3,1024,512]{1,2,0:T(8,128)} fusion(bf16[3,1024,512]{2,1,0:T(8,128)(2,1)} %constant_dynamic-update-slice_fusion, f32[1024]{0:T(1024)S(1)} %copy-done.23, bf16[1024,1024]{1,0:T(8,128)(2,1)} %param.7, f32[1024]{0:T(1024)S(1)} %add_rsqrt_fusion, f32[1024]{0:T(1024)S(1)} %copy-done.19), kind=kOutput, calls=%fused_computation.12 | convolution fusion | flops 3226468352 | bytes 11546624 | tf_op jit(solution)/shard_map/rd,mrh->mdh/dot_general | solution.py:161
  195.1 11.3 %fusion.30 = bf16[34,32,4,128]{3,1,2,0:T(8,128)(2,1)} fusion(bf16[34,96,4,128]{3,1,2,0:T(8,128)(2,1)} %copy-done.7, f32[34,4,32]{2,1,0:T(4,128)S(1)} %get-tuple-element.41, f32[34,4,32,96]{3,2,1,0:T(8,128)} %copy-done.5, pred[34,32,96]{2,1,0:T(8,128)(4,1)S(1)} %or_and_fusion), kind=kOutput, calls=%fused_computation.41 | convolution fusion | flops 109605216 | bytes 6249472 | tf_op jit(solution)/shard_map/chij,cjhd->cihd/dot_general | solution.py:95
  208.4 2.7 fusion.15
  211.1 84.6 %all-reduce.9.cloned.1.call-done = f32[1024,1024]{1,0:T(8,128)} async-done(((f32[1024,1024]{1,0:T(8,128)}), f32[1024,1024]{1,0:T(8,128)}) %all-reduce.9.cloned.1.call-update) | async-done | bytes 4194320 | tf_op jit(solution)/shard_map/psum | solution.py:168
  295.6 3.9 %fusion.64 = (f32[1024]{0:T(1024)S(1)}, f32[1024]{0:T(1024)S(1)}, f32[1024,1024]{1,0:T(8,128)S(1)}, f32[1024,1024]{1,0:T(8,128)S(1)}) fusion(f32[1024]{0:T(1024)S(1)} %add_rsqrt_fusion, f32[1024]{0:T(1024)S(1)} %copy-done.19, bf16[1024,1024]{1,0:T(8,128)(2,1)} %param.7, f32[1024,1024]{1,0:T(8,128)} %all-reduce.9.cloned.1.call-done, f32[1024]{0:T(1024)S(1)} %copy-done.23), kind=kLoop, calls=%fused_computation.109 | loop fusion | flops 7337984 | bytes 14700544 | tf_op jit(solution)/shard_map/reduce_sum | solution.py:34
  301.0 2.3 copy.53
  (108 shorter events, 34.4 us)
Async XLA Ops:
  8.0 6.5 %copy-start = (bf16[3,1024,512]{2,1,0:T(8,128)(2,1)S(1)}, bf16[3,1024,512]{2,1,0:T(8,128)(2,1)}, u32[]{:S(2)}) copy-start(bf16[3,1024,512]{2,1,0:T(8,128)(2,1)} %param.9) | copy-start | bytes 9437188
  8.0 287.6 %all-reduce.9.cloned.1.call-start = ((), (), s32[]{:S(2)}) async-start(), calls=%async_computation.2 | async-start | bytes 8388608 | tf_op jit(solution)/shard_map/psum | solution.py:168
  8.1 2.4 copy-start.2
  8.1 3.1 copy-start.17
  10.4 4.1 %copy-start.18 = (f32[1024]{0:T(1024)}, f32[1024]{0:T(1024)S(1)}, u32[]{:S(2)}) copy-start(f32[1024]{0:T(1024)S(1)} %broadcast_multiply_fusion.3) | copy-start | bytes 12292
  11.2 3.4 %copy-start.20 = (bf16[1024]{0:T(1024)(128)(2,1)}, bf16[1024]{0:T(1024)(128)(2,1)S(1)}, u32[]{:S(2)}) copy-start(bf16[1024]{0:T(1024)(128)(2,1)S(1)} %dynamic-slice_convert_fusion) | copy-start | bytes 6148
  11.2 3.4 %copy-start.3 = (bf16[1024,1024]{1,0:T(8,128)(2,1)S(1)}, bf16[1024,1024]{1,0:T(8,128)(2,1)}, u32[]{:S(2)}) copy-start(bf16[1024,1024]{1,0:T(8,128)(2,1)} %param.7) | copy-start | bytes 6291460
  11.2 3.4 %copy-start.22 = (f32[1024]{0:T(1024)S(1)}, f32[1024]{0:T(1024)}, u32[]{:S(2)}) copy-start(f32[1024]{0:T(1024)} %param.8) | copy-start | bytes 12292
  14.6 4.0 %copy-start.4 = (bf16[1,1024,512]{2,1,0:T(8,128)(2,1)}, bf16[1,1024,512]{2,1,0:T(8,128)(2,1)S(1)}, u32[]{:S(2)}) copy-start(bf16[1,1024,512]{2,1,0:T(8,128)(2,1)S(1)} %fusion.34) | copy-start | bytes 3145732
  18.6 1.8 copy-start.1
  18.6 7.5 %copy-start.24 = (s32[8]{0:T(128)S(1)}, s32[8]{0:T(128)}, u32[]{:S(2)}) copy-start(s32[8]{0:T(128)} %param.13) | copy-start | bytes 100
  20.4 13.0 %collective-permute-start.1 = (bf16[4,64,512]{2,1,0:T(8,128)(2,1)}, bf16[4,64,512]{2,1,0:T(8,128)(2,1)S(1)}, u32[]{:S(2)}, u32[]{:S(2)}) collective-permute-start(bf16[4,64,512]{2,1,0:T(8,128)(2,1)} %get-tuple-element.29), channel_id=1, source_target_pairs={{4,0},{8,4},{12,8},{16,12},{20,16},{24,20},{28,24},{5,1},{9,5},{13... | collective-permute-start | bytes 786440 | tf_op jit(solution)/shard_map/ppermute | solution.py:19
  21.7 11.7 %collective-permute-start = (bf16[4,64,512]{2,1,0:T(8,128)(2,1)}, bf16[4,64,512]{2,1,0:T(8,128)(2,1)}, u32[]{:S(2)}, u32[]{:S(2)}) collective-permute-start(bf16[4,64,512]{2,1,0:T(8,128)(2,1)} %get-tuple-element.30), channel_id=1, source_target_pairs={{0,4},{4,8},{8,12},{12,16},{16,20},{20,24},{24,28},{1,5},{5,9},{9,... | collective-permute-start | bytes 786440 | tf_op jit(solution)/shard_map/ppermute | solution.py:16
  65.6 1.6 copy-start.14
  65.6 1.9 copy-start.13
  67.3 1.3 copy-start.10
  67.5 1.4 copy-start.8
  68.9 3.2 %copy-start.7 = (bf16[34,96,4,128]{3,1,2,0:T(8,128)(2,1)}, bf16[34,96,4,128]{3,1,2,0:T(8,128)(2,1)S(1)}, u32[]{:S(2)}) copy-start(bf16[34,96,4,128]{3,1,2,0:T(8,128)(2,1)S(1)} %copy_dynamic-update-slice_fusion) | copy-start | bytes 10027012
  69.0 3.2 %copy-start.11 = (bf16[34,32,4,128]{3,2,1,0:T(4,128)(2,1)S(1)}, bf16[34,32,4,128]{3,2,1,0:T(4,128)(2,1)}, u32[]{:S(2)}) copy-start(bf16[34,32,4,128]{3,2,1,0:T(4,128)(2,1)} %slice.194) | copy-start | bytes 3342340
  72.2 1.2 copy-start.12
  72.2 1.6 copy-start.9
  73.8 1.8 copy-start.6
  75.6 2.2 copy-start.5
  151.0 1.2 slice-start
  175.2 2.4 copy-start.15
  185.5 0.7 copy-start.19
  185.5 0.7 copy-start.23
  185.5 115.5 %reduce-scatter.3.cloned.1.call-start = ((), (), s32[]{:S(2)}) async-start(), calls=%async_computation.3 | async-start | bytes 7077888 | tf_op jit(solution)/shard_map/reduce_scatter | solution.py:164
  195.0 109.2 %reduce-scatter.5.cloned.1.call-start = ((), (), s32[]{:S(2)}) async-start(), calls=%async_computation.4 | async-start | bytes 2359296 | tf_op jit(solution)/shard_map/reduce_scatter | solution.py:165
  206.4 1.2 slice-start.1
  206.4 2.0 copy-start.16
  206.4 2.0 copy-start.21
Sparse Core Ops, SparseCore 0:
  185.6 109.9 all-reduce.8
Sparse Core Ops, SparseCore 1:
  195.1 71.6 reduce-scatter.2
  269.5 34.7 reduce-scatter.4
where the time goes:
time: 317 us; the launch traced here: 312 us
  matrix products  115 us (36%)
  waiting for transfers between devices  85.6 us (27%)
  local copies, waits for them, and re-layouts  64.8 us (20%)
  other arithmetic  24.9 us (8%)
  between operations  16.1 us (5%)
  starting transfers between devices  5.15 us (2%)
    psum x1, waiting for transfers between devices, on_device(): head_total = lax.psum(incoming, 'mp')  84.6 us
    dot_general x1, matrix products, attend(): jnp.einsum('chij,cihd->cjhd', score_grad, queries, preferred_element_type...  31.5 us
    dot_general x1, matrix products, attend(): jnp.einsum('chij,cjhd->cihd', score_grad, key_win, preferred_element_type...  28.3 us
    dot_general x1, matrix products, attend(): jnp.einsum('chij,cihd->cjhd', rounded, grad_rows, preferred_element_type=...  13.4 us
    unnamed x57, local copies, waits for them, and re-layouts  13.1 us
    dot_general x1, matrix products, attend(): jnp.einsum('chij,cjhd->cihd', rounded, value_win, preferred_element_type=...  11.3 us
    dot_general x1, matrix products, on_device(): jnp.einsum('rd,mrh->mdh', normed, all_grads, preferred_element_type=jnp.f...  8.83 us
    another operation x4, local copies, waits for them, and re-layouts, on_device(): jnp.stack([query_grad, key_grad, value_grad])  8 us
  transfers between devices with their start and end apart: 5, of which 2 were waited for; matrix products, arithmetic and copies ran while one was open for 12% of the time, Pallas kernels for 0%

commit v1 on v0

--- a/solution.py
+++ b/solution.py
@@ -165,7 +165,8 @@
         lax.psum_scatter(out_terms, "tm", scatter_dimension=1, tiled=True),
     )
     incoming = jnp.einsum("mrh,mdh->rd", all_grads, qkv_weight, preferred_element_type=jnp.float32)
-    head_total = lax.psum(incoming, "mp")
+    theirs = lax.ppermute(incoming, "mp", [(0, 1), (1, 0)])
+    head_total = incoming + theirs
     full_grad = norm_backward(head_total, normal_form, inverse, norm_gain)
     share_cols = full_grad.shape[1] // lax.axis_size("mp")
     frame_grad = lax.dynamic_slice_in_dim(

time: 317 us -> 316 us (level)
  waiting for transfers between devices: 85.6 us -> 75.8 us
  local copies, waits for them, and re-layouts: 64.8 us -> 71.9 us
    psum x1 -> x0, waiting for transfers between devices: 84.6 us -> none  [on_device(): head_total = lax.psum(incoming, 'mp')]
    ppermute x0 -> x1, waiting for transfers between devices: none -> 75.8 us  [on_device(): theirs = lax.ppermute(incoming, 'mp', [(0, 1), (1, 0)])]
    unnamed x57 -> x59, local copies, waits for them, and re-layouts: 13.1 us -> 18.8 us
  transfers between devices with their start and end apart: 5 -> 5, of which waited for: 2 -> 1; matrix products, arithmetic and copies ran while one was open for 12% -> 13% of each run, Pallas kernels for 0% -> 0%
where the time goes in v1:
time: 316 us; the launch traced here: 311 us
  matrix products  114 us (36%)
  waiting for transfers between devices  75.8 us (24%)
  local copies, waits for them, and re-layouts  71.9 us (23%)
  other arithmetic  26.1 us (8%)
  between operations  14.7 us (5%)
  starting transfers between devices  8.11 us (3%)
    ppermute x1, waiting for transfers between devices, on_device(): theirs = lax.ppermute(incoming, 'mp', [(0, 1), (1, 0)])  75.8 us
    dot_general x1, matrix products, attend(): jnp.einsum('chij,cihd->cjhd', score_grad, queries, preferred_element_type...  31.5 us
    dot_general x1, matrix products, attend(): jnp.einsum('chij,cjhd->cihd', score_grad, key_win, preferred_element_type...  28.3 us
    unnamed x59, local copies, waits for them, and re-layouts  18.8 us
    dot_general x1, matrix products, attend(): jnp.einsum('chij,cihd->cjhd', rounded, grad_rows, preferred_element_type=...  13.4 us
    dot_general x1, matrix products, attend(): jnp.einsum('chij,cjhd->cihd', rounded, value_win, preferred_element_type=...  11.3 us
    another operation x4, local copies, waits for them, and re-layouts, on_device(): jnp.stack([query_grad, key_grad, value_grad])  9.29 us
    dot_general x1, matrix products, on_device(): jnp.einsum('rd,mrh->mdh', normed, all_grads, preferred_element_type=jnp.f...  7.78 us
  transfers between devices with their start and end apart: 5, of which 1 were waited for; matrix products, arithmetic and copies ran while one was open for 13% of the time, Pallas kernels for 0%

profile of v1, /device:TPU:0, one launch (start us, length us, event | category | flops | bytes accessed | tf_op | source)
XLA Modules:
  0.0 310.7 jit_solution(18368102848599103037)
XLA Ops:
  7.2 4.1 %copy.46 = bf16[1024,1024]{0,1:T(8,128)(2,1)} copy(bf16[1024,1024]{1,0:T(8,128)(2,1)} %param.7) | data formatting | bytes 4194304 | tf_op args[0]
  14.3 3.3 %fusion.34 = bf16[1,1024,512]{2,1,0:T(8,128)(2,1)S(1)} fusion(bf16[512,1024]{1,0:T(8,128)(2,1)} %param.10, bf16[1024,1024]{1,0:T(8,128)(2,1)} %param.11, bf16[1024]{0:T(1024)(128)(2,1)S(1)} %dynamic-slice_convert_fusion), kind=kOutput, calls=%fused_computation.43 | convolution fusion | flops 1075314688 | bytes 4196352 | tf_op jit(solution)/shard_map/dot_general | solution.py:126
  17.6 3.9 %convert_bitcast_fusion = bf16[3,1024,512]{2,1,0:T(8,128)(2,1)S(1)} fusion(bf16[3,1024,512]{2,1,0:T(8,128)(2,1)S(1)} %copy-done, f32[1024]{0:T(1024)S(1)} %copy-done.22, f32[1024]{0:T(1024)S(1)} %add_rsqrt_fusion, f32[1024]{0:T(1024)S(1)} %broadcast_multiply_fusion.2, bf16[1024,1024]{0,1:T(8,128)(2,1)S(1)} %copy-done.2), kind=kOutput, calls=%fused_computation.10 | convolution fusion | flops 3228041216 | bytes 8400896 | tf_op jit(solution)/shard_map/rd,mdh->mrh/dot_general | solution.py:121
  24.6 3.8 %collective-permute-start = (bf16[4,64,512]{2,1,0:T(8,128)(2,1)}, bf16[4,64,512]{2,1,0:T(8,128)(2,1)}, u32[]{:S(2)}, u32[]{:S(2)}) collective-permute-start(bf16[4,64,512]{2,1,0:T(8,128)(2,1)} %get-tuple-element.30), channel_id=1, source_target_pairs={{0,4},{4,8},{8,12},{12,16},{16,20},{20,24},{24,28},{1,5},{5,9},{9,... | collective-permute-start | bytes 786440 | tf_op jit(solution)/shard_map/ppermute | solution.py:16
  36.4 3.2 %pad_maximum_fusion = (bf16[1,1088,512]{2,1,0:T(8,128)(2,1)}, bf16[1,1088,512]{2,1,0:T(8,128)(2,1)}, bf16[1,1088,512]{2,1,0:T(8,128)(2,1)}) fusion(bf16[4,64,512]{2,1,0:T(8,128)(2,1)S(1)} %collective-permute-done.1, bf16[1,1024,512]{2,1,0:T(8,128)(2,1)} %copy-done.5, bf16[3,1024,512]{2,1,0:T(8,128)(2,1)} %copy-done.4, ...), kind=kLoop, calls=%fused_computation.44 | loop fusion | flops 10027008 | bytes 8060928 | tf_op jit(solution)/shard_map/concatenate | solution.py:20
  39.6 3.1 slice.216
  42.7 4.3 %pad_maximum_fusion.11 = (bf16[1,1088,512]{2,1,0:T(8,128)(2,1)}, bf16[1,1088,512]{2,1,0:T(8,128)(2,1)}, bf16[1,1088,512]{2,1,0:T(8,128)(2,1)}, bf16[1,1088,512]{2,1,0:T(8,128)(2,1)}, bf16[1,1088,512]{2,1,0:T(8,128)(2,1)}) fusion(bf16[4,64,512]{2,1,0:T(8,128)(2,1)S(1)} %collective-permute-done.1, bf16[4,64,512]{2,1,0:T(8,128)(2,1)} %collective-permute-done, ...), kind=kLoop, calls=%fused_computation.55 | loop fusion | flops 21168128 | bytes 10289152 | tf_op jit(solution)/shard_map/slice | solution.py:145
  47.1 3.1 reshape_squeeze.8
  50.1 3.1 reshape_squeeze.9
  53.3 3.1 slice.194
  56.3 3.1 slice.214
  59.4 3.1 slice.191
  62.5 3.1 slice.196
  65.6 3.1 slice.212
  72.1 3.2 %fusion.47 = f32[34,4,32,96]{3,2,1,0:T(8,128)} fusion(bf16[34,96,4,128]{3,1,2,0:T(8,128)(2,1)S(1)} %copy_dynamic-update-slice_fusion, bf16[34,32,4,128]{3,2,1,0:T(4,128)(2,1)S(1)} %copy-done.9), kind=kOutput, calls=%fused_computation.73 | convolution fusion | flops 106954752 | bytes 6127616 | tf_op jit(solution)/shard_map/cihd,cjhd->chij/dot_general | solution.py:98
  80.9 28.3 %fusion.31 = bf16[34,32,4,128]{3,1,2,0:T(8,128)(2,1)} fusion(bf16[34,96,4,128]{3,1,2,0:T(8,128)(2,1)} %copy-done.7, f32[34,4,32,96]{3,2,1,0:T(8,128)} %fusion.47, f32[34,4,32,96]{3,2,1,0:T(8,128)} %get-tuple-element.42, f32[34,4,32]{2,1,0:T(4,128)S(1)} %get-tuple-element.41), kind=kOutput, calls=%fused_computation.42 | convolution fusion | flops 110440800 | bytes 7816192 | tf_op jit(solution)/shard_map/chij,cjhd->cihd/dot_general | solution.py:103
  109.3 31.5 %convolution_bitcast_fusion.1 = f32[34,96,4,128]{3,1,2,0:T(8,128)} fusion(f32[34,4,32,96]{3,2,1,0:T(8,128)} %fusion.47, bf16[34,32,4,128]{3,2,1,0:T(4,128)(2,1)} %reshape_squeeze.8, f32[34,4,32,96]{3,2,1,0:T(8,128)} %get-tuple-element.42, f32[34,4,32]{2,1,0:T(4,128)S(1)} %get-tuple-element.41), kind=kOutput, calls=%fused_computation.12 | convolution fusion | flops 109883744 | bytes 11158528 | tf_op jit(solution)/shard_map/chij,cihd->cjhd/dot_general | solution.py:107
  140.8 13.4 %convolution_bitcast_fusion = f32[34,96,4,128]{3,1,2,0:T(8,128)} fusion(bf16[34,32,4,128]{3,2,1,0:T(4,128)(2,1)} %reshape_squeeze.9, f32[34,4,32]{2,1,0:T(4,128)S(1)} %get-tuple-element.41, f32[34,4,32,96]{3,2,1,0:T(8,128)} %copy-done.6, pred[34,32,96]{2,1,0:T(8,128)(4,1)S(1)} %or_and_fusion), kind=kOutput, calls=%fused_computation.11 | convolution fusion | flops 109048160 | bytes 9591808 | tf_op jit(solution)/shard_map/chij,cihd->cjhd/dot_general | solution.py:110
  156.9 2.3 stack.12
  159.2 3.8 %fusion.64 = (f32[34,32,4,128]{3,1,2,0:T(8,128)S(1)}, f32[34,32,4,128]{3,1,2,0:T(8,128)S(1)}, f32[34,32,4,128]{3,1,2,0:T(8,128)S(1)}) fusion(f32[34,96,4,128]{3,1,2,0:T(8,128)} %convolution_bitcast_fusion.1), kind=kLoop, calls=%fused_computation.111 | loop fusion | bytes 13369344 | tf_op jit(solution)/shard_map/slice | solution.py:51
  167.6 2.3 constant_dynamic-update-slice_fusion.2
  169.8 3.8 %fusion.63 = (f32[34,32,4,128]{3,1,2,0:T(8,128)S(1)}, f32[34,32,4,128]{3,1,2,0:T(8,128)S(1)}, f32[34,32,4,128]{3,1,2,0:T(8,128)S(1)}) fusion(f32[34,96,4,128]{3,1,2,0:T(8,128)} %convolution_bitcast_fusion), kind=kLoop, calls=%fused_computation.110 | loop fusion | bytes 13369344 | tf_op jit(solution)/shard_map/slice | solution.py:51
  175.9 2.4 stack.14
  178.4 2.4 constant_dynamic-update-slice_fusion.1
  180.8 2.3 constant_dynamic-update-slice_fusion
  183.1 7.8 %convolution_bitcast_fusion.2 = f32[3,1024,512]{1,2,0:T(8,128)} fusion(bf16[3,1024,512]{2,1,0:T(8,128)(2,1)} %constant_dynamic-update-slice_fusion, f32[1024]{0:T(1024)S(1)} %copy-done.23, f32[1024]{0:T(1024)S(1)} %add_rsqrt_fusion, f32[1024]{0:T(1024)S(1)} %copy-done.19, bf16[1024,1024]{0,1:T(8,128)(2,1)S(1)} %copy-done.3), kind=kOutput, calls=%fused_computation.13 | convolution fusion | flops 3226468352 | bytes 11546624 | tf_op jit(solution)/shard_map/rd,mrh->mdh/dot_general | solution.py:161
  191.0 6.9 %convolution_bitcast_fusion.3 = f32[1024,1024]{0,1:T(8,128)} fusion(bf16[3,1024,512]{2,1,0:T(8,128)(2,1)} %constant_dynamic-update-slice_fusion, bf16[3,1024,512]{2,1,0:T(8,128)(2,1)S(1)} %copy-done), kind=kOutput, calls=%fused_computation.19 | convolution fusion | flops 3221225472 | bytes 10485760 | tf_op jit(solution)/shard_map/mrh,mdh->rd/dot_general | solution.py:167
  197.9 3.0 collective-permute-start.2
  200.9 11.3 %fusion.30 = bf16[34,32,4,128]{3,1,2,0:T(8,128)(2,1)} fusion(bf16[34,96,4,128]{3,1,2,0:T(8,128)(2,1)} %copy-done.8, f32[34,4,32]{2,1,0:T(4,128)S(1)} %get-tuple-element.41, f32[34,4,32,96]{3,2,1,0:T(8,128)} %copy-done.6, pred[34,32,96]{2,1,0:T(8,128)(4,1)S(1)} %or_and_fusion), kind=kOutput, calls=%fused_computation.41 | convolution fusion | flops 109605216 | bytes 6249472 | tf_op jit(solution)/shard_map/chij,cjhd->cihd/dot_general | solution.py:95
  214.1 2.7 fusion.15
  216.8 75.8 %collective-permute-done.2 = f32[1024,1024]{0,1:T(8,128)} collective-permute-done((f32[1024,1024]{0,1:T(8,128)}, f32[1024,1024]{0,1:T(8,128)}, u32[]{:S(2)}, u32[]{:S(2)}) %collective-permute-start.2) | collective-permute-done | bytes 4194336 | tf_op jit(solution)/shard_map/ppermute | solution.py:168
  292.6 5.0 %fusion.62 = (f32[1024]{0:T(1024)S(1)}, f32[1024]{0:T(1024)S(1)}, f32[1024,1024]{0,1:T(8,128)S(1)}, f32[1024,1024]{0,1:T(8,128)S(1)}) fusion(f32[1024]{0:T(1024)S(1)} %add_rsqrt_fusion, f32[1024]{0:T(1024)S(1)} %copy-done.19, bf16[1024,1024]{0,1:T(8,128)(2,1)} %copy.46, f32[1024]{0:T(1024)S(1)} %copy-done.23, f32[1024,1024]{0,1:T(8,128)} %convolution_bitcast_fusion.3, ...), kind=kLoop, calls=%fused_computation.109 | loop fusion | flops 8386560 | bytes 18894848 | tf_op jit(solution)/shard_map/reduce_sum | solution.py:34
  (109 shorter events, 40.5 us)
Async XLA Ops:
  7.2 10.4 %copy-start = (bf16[3,1024,512]{2,1,0:T(8,128)(2,1)S(1)}, bf16[3,1024,512]{2,1,0:T(8,128)(2,1)}, u32[]{:S(2)}) copy-start(bf16[3,1024,512]{2,1,0:T(8,128)(2,1)} %param.9) | copy-start | bytes 9437188
  7.2 294.2 %reduce-scatter.3.cloned.1.call-start = ((), (), s32[]{:S(2)}) async-start(), calls=%async_computation.2 | async-start | bytes 7077888 | tf_op jit(solution)/shard_map/reduce_scatter | solution.py:164
  11.4 2.2 copy-start.1
  11.4 2.8 copy-start.17
  13.6 4.0 %copy-start.18 = (f32[1024]{0:T(1024)}, f32[1024]{0:T(1024)S(1)}, u32[]{:S(2)}) copy-start(f32[1024]{0:T(1024)S(1)} %broadcast_multiply_fusion.2) | copy-start | bytes 12292
  14.2 3.4 %copy-start.20 = (bf16[1024]{0:T(1024)(128)(2,1)}, bf16[1024]{0:T(1024)(128)(2,1)S(1)}, u32[]{:S(2)}) copy-start(bf16[1024]{0:T(1024)(128)(2,1)S(1)} %dynamic-slice_convert_fusion) | copy-start | bytes 6148
  14.2 3.4 %copy-start.2 = (bf16[1024,1024]{0,1:T(8,128)(2,1)S(1)}, bf16[1024,1024]{0,1:T(8,128)(2,1)}, u32[]{:S(2)}) copy-start(bf16[1024,1024]{0,1:T(8,128)(2,1)} %copy.46) | copy-start | bytes 6291460
  14.3 3.4 %copy-start.22 = (f32[1024]{0:T(1024)S(1)}, f32[1024]{0:T(1024)}, u32[]{:S(2)}) copy-start(f32[1024]{0:T(1024)} %param.8) | copy-start | bytes 12292
  17.6 3.9 %copy-start.5 = (bf16[1,1024,512]{2,1,0:T(8,128)(2,1)}, bf16[1,1024,512]{2,1,0:T(8,128)(2,1)S(1)}, u32[]{:S(2)}) copy-start(bf16[1,1024,512]{2,1,0:T(8,128)(2,1)S(1)} %fusion.34) | copy-start | bytes 3145732
  21.6 1.8 copy-start.4
  21.6 7.5 %copy-start.24 = (s32[8]{0:T(128)S(1)}, s32[8]{0:T(128)}, u32[]{:S(2)}) copy-start(s32[8]{0:T(128)} %param.13) | copy-start | bytes 100
  23.4 13.0 %collective-permute-start.1 = (bf16[4,64,512]{2,1,0:T(8,128)(2,1)}, bf16[4,64,512]{2,1,0:T(8,128)(2,1)S(1)}, u32[]{:S(2)}, u32[]{:S(2)}) collective-permute-start(bf16[4,64,512]{2,1,0:T(8,128)(2,1)} %get-tuple-element.29), channel_id=1, source_target_pairs={{4,0},{8,4},{12,8},{16,12},{20,16},{24,20},{28,24},{5,1},{9,5},{13... | collective-permute-start | bytes 786440 | tf_op jit(solution)/shard_map/ppermute | solution.py:19
  24.6 11.8 %collective-permute-start = (bf16[4,64,512]{2,1,0:T(8,128)(2,1)}, bf16[4,64,512]{2,1,0:T(8,128)(2,1)}, u32[]{:S(2)}, u32[]{:S(2)}) collective-permute-start(bf16[4,64,512]{2,1,0:T(8,128)(2,1)} %get-tuple-element.30), channel_id=1, source_target_pairs={{0,4},{4,8},{8,12},{12,16},{16,20},{20,24},{24,28},{1,5},{5,9},{9,... | collective-permute-start | bytes 786440 | tf_op jit(solution)/shard_map/ppermute | solution.py:16
  68.7 1.6 copy-start.15
  68.7 1.9 copy-start.14
  70.4 1.3 copy-start.11
  70.6 1.4 copy-start.9
  72.1 3.2 %copy-start.8 = (bf16[34,96,4,128]{3,1,2,0:T(8,128)(2,1)}, bf16[34,96,4,128]{3,1,2,0:T(8,128)(2,1)S(1)}, u32[]{:S(2)}) copy-start(bf16[34,96,4,128]{3,1,2,0:T(8,128)(2,1)S(1)} %copy_dynamic-update-slice_fusion) | copy-start | bytes 10027012
  72.1 3.2 %copy-start.12 = (bf16[34,32,4,128]{3,2,1,0:T(4,128)(2,1)S(1)}, bf16[34,32,4,128]{3,2,1,0:T(4,128)(2,1)}, u32[]{:S(2)}) copy-start(bf16[34,32,4,128]{3,2,1,0:T(4,128)(2,1)} %slice.194) | copy-start | bytes 3342340
  75.3 1.2 copy-start.13
  75.3 1.6 copy-start.10
  76.9 1.8 copy-start.7
  78.7 2.2 copy-start.6
  154.2 1.2 slice-start
  178.4 4.7 %copy-start.3 = (bf16[1024,1024]{0,1:T(8,128)(2,1)S(1)}, bf16[1024,1024]{0,1:T(8,128)(2,1)}, u32[]{:S(2)}) copy-start(bf16[1024,1024]{0,1:T(8,128)(2,1)} %copy.46) | copy-start | bytes 6291460
  178.4 4.7 %copy-start.19 = (f32[1024]{0:T(1024)S(1)}, f32[1024]{0:T(1024)}, u32[]{:S(2)}) copy-start(f32[1024]{0:T(1024)} %copy-done.18) | copy-start | bytes 12292
  178.4 4.7 %copy-start.23 = (f32[1024]{0:T(1024)S(1)}, f32[1024]{0:T(1024)}, u32[]{:S(2)}) copy-start(f32[1024]{0:T(1024)} %param.8) | copy-start | bytes 12292
  190.9 112.7 %reduce-scatter.5.cloned.1.call-start = ((), (), s32[]{:S(2)}) async-start(), calls=%async_computation.3 | async-start | bytes 2359296 | tf_op jit(solution)/shard_map/reduce_scatter | solution.py:165
  197.9 94.7 %collective-permute-start.2 = (f32[1024,1024]{0,1:T(8,128)}, f32[1024,1024]{0,1:T(8,128)}, u32[]{:S(2)}, u32[]{:S(2)}) collective-permute-start(f32[1024,1024]{0,1:T(8,128)} %convolution_bitcast_fusion.3), channel_id=1, source_target_pairs={{0,2},{2,0},{1,3},{3,1},{4,6},{6,4},{5,7},{7,5},{8,10},{10,8},{9,1... | collective-permute-start | bytes 12582920 | tf_op jit(solution)/shard_map/ppermute | solution.py:168
  212.2 1.2 slice-start.1
  212.2 1.9 copy-start.16
  212.2 1.9 copy-start.21
Sparse Core Ops, SparseCore 0:
  191.0 71.7 reduce-scatter.2
  265.7 34.4 reduce-scatter.4
